TPU v7x, 128 devices: a whole 4x4x4 slice. The times are simulated.
128 devices in a mesh: grp: 8 (over y, core), hlp: 16 (over z, x).
Axes of the slice: x: 4, y: 4, z: 4, core: 2. Of those that a mesh axis runs over, the one named last changes fastest.
Arguments:
- pivot_inverse: bfloat16 [8, 2048, 2048], P('grp', 'hlp'), may hold values from -1 to 2, as said below
- cross_block: bfloat16 [8, 3584, 2048], P('grp', 'hlp'), may hold values from -0.375 to 0.375
- contrib_block: float32 [8, 3584, 3584], P('grp', 'hlp'), may hold values from -3 to 3, as said below
- pivot_sources: bfloat16 [8, 2048, 512], P('grp', 'hlp'), may hold values from -6 to 6
- contrib_sources: bfloat16 [8, 3584, 512], P('grp', 'hlp'), may hold values from -6 to 6
- ext_map: int32 [8, 3584], P('grp', 'hlp'), may hold values from 0 to 7167, as said below
- parent_front: float32 [7168, 7168], P(('grp', 'hlp')), may hold values from -6 to 6, as said below
- parent_rhs: float32 [7168, 512], P(('grp', 'hlp')), may hold values from -6 to 6
Outputs:
- solved: bfloat16 [8, 2048, 512], P('grp', 'hlp')
- front_out: float32 [7168, 7168], P(('grp', 'hlp'))
- rhs_out: float32 [7168, 512], P(('grp', 'hlp'))
Inputs may be any that keep to these rules, and one draw needn't show every extreme that they name: `ext_map`: the 3584 entries of one child are distinct. Within each aligned block of 224 entries of a child, at most 3 entries fall into any one aligned block of 56 parent rows, and exactly 3 fall into some such block. `pivot_inverse`: lower triangular with positive diagonal. `contrib_block`: each child's block is symmetric. `parent_front`: Symmetric.
All inputs are finite; a program needn't handle non-finite values.
Results may differ from a plain program's by a relative error of at most 0.0043.
Values may be sent and summed in bfloat16 or wider, within the bound.
A program may use at most 128 MiB of HBM per device.

v0:
```python
import jax
import jax.numpy as jnp
from jax import lax
from jax.sharding import PartitionSpec as P


def joined_along(pieces, dim):
    dims = list(pieces.shape[1:])
    dims[dim] *= pieces.shape[0]
    return jnp.moveaxis(pieces, 0, dim).reshape(dims)


def sent_to_all(value, axis):
    copies = jnp.broadcast_to(value, (lax.axis_size(axis), *value.shape))
    return lax.all_to_all(copies, axis, split_axis=0, concat_axis=0, tiled=True)


def gathered_copies(value, axis, dim):
    return joined_along(sent_to_all(value, axis), dim)


def sent_together(arrays, axis, split_dim, concat_dim, along):
    columns = [a.reshape(*a.shape[:along], -1) for a in arrays]
    both = jnp.concatenate(columns, axis=along)
    filled, at, finished = (
        lax.all_to_all(both, axis, split_axis=split_dim, concat_axis=concat_dim, tiled=True),
        0,
        [],
    )
    for a, column in zip(arrays, columns):
        slab = filled[..., at : at + column.shape[along]]
        finished.append(slab.reshape(*slab.shape[:along], *a.shape[along:]))
        at += column.shape[along]
    return tuple(finished)


def on_device(
    pivot_inverse,
    cross_block,
    contrib_block,
    pivot_sources,
    contrib_sources,
    ext_map,
    parent_front,
    parent_rhs,
):
    inverse = pivot_inverse[0]
    coupling = cross_block[0]
    contrib_rows = contrib_block[0].shape[1]
    helpers = lax.axis_size("hlp")
    groups = lax.axis_size("grp")
    devices = helpers * groups
    capacity = max(1, 2 * contrib_rows // (helpers * devices))
    owned = parent_front.shape[0]
    parent_width = parent_front.shape[1]
    source_width = pivot_sources.shape[2]
    lower_part = jnp.einsum(
        "rp,np->rn",
        coupling,
        lax.all_gather(inverse, "hlp", axis=0, tiled=True),
        preferred_element_type=jnp.float32,
    ).astype(jnp.bfloat16)
    schur_rows = contrib_block[0] - jnp.einsum(
        "rp,np->rn",
        lower_part,
        lax.all_gather(lower_part, "hlp", axis=0, tiled=True),
        preferred_element_type=jnp.float32,
    )
    block = inverse
    solved = jnp.dot(
        block, gathered_copies(pivot_sources[0], "hlp", 0), preferred_element_type=jnp.float32
    ).astype(jnp.bfloat16)
    block = lower_part
    update = contrib_sources[0].astype(jnp.float32) - jnp.dot(
        block, gathered_copies(solved, "hlp", 0), preferred_element_type=jnp.float32
    )
    local_map = ext_map[0]
    local_rows = local_map.shape[0]
    owners = local_map // owned
    local_row = local_map % owned
    one_hot = (owners[:, None] == jnp.arange(devices)[None, :]).astype(jnp.int32)
    earlier = jnp.cumsum(one_hot, axis=0) - one_hot
    position = jnp.sum(earlier * one_hot, axis=1)
    slot_index = owners * capacity + position
    full_map = gathered_copies(ext_map, "hlp", 1)[0]
    payload = jnp.zeros((local_rows, parent_width), jnp.float32).at[:, full_map].set(schur_rows)
    row_width = payload.shape[1]
    send_rows = jnp.zeros((devices * capacity, row_width), jnp.float32).at[slot_index].set(payload)
    send_rhs = jnp.zeros((devices * capacity, source_width), jnp.float32).at[slot_index].set(update)
    targets = (
        jnp.full((devices * capacity,), -1.0, jnp.float32)
        .at[slot_index]
        .set(local_row.astype(jnp.float32))
    )
    received = tuple(
        (
            part.astype(jnp.float32)
            for part in sent_together(
                (
                    send_rows.reshape(devices, capacity, row_width).astype(jnp.bfloat16),
                    send_rhs.reshape(devices, capacity, source_width).astype(jnp.bfloat16),
                    targets.reshape(devices, capacity).astype(jnp.bfloat16),
                ),
                ("grp", "hlp"),
                0,
                0,
                2,
            )
        )
    )
    rows_in = received[0].reshape(devices * capacity, row_width)
    rhs_in = received[1].reshape(devices * capacity, source_width)
    targets_in = received[2].reshape(devices * capacity)
    row_index = jnp.where(targets_in < 0.0, owned, targets_in).astype(jnp.int32)
    front_out = (
        parent_front
        + jnp.zeros((owned + 1, parent_width), jnp.float32).at[row_index].add(rows_in)[:owned]
    )
    rhs_out = (
        parent_rhs
        + jnp.zeros((owned + 1, source_width), jnp.float32).at[row_index].add(rhs_in)[:owned]
    )
    return (solved[None], front_out, rhs_out)


def solution(mesh):
    return jax.shard_map(
        on_device,
        mesh=mesh,
        in_specs=(
            P("grp", "hlp", None),
            P("grp", "hlp", None),
            P("grp", "hlp", None),
            P("grp", "hlp", None),
            P("grp", "hlp", None),
            P("grp", "hlp"),
            P(("grp", "hlp"), None),
            P(("grp", "hlp"), None),
        ),
        out_specs=(P("grp", "hlp", None), P(("grp", "hlp"), None), P(("grp", "hlp"), None)),
        check_vma=False,
    )
```

profile of v0, /device:TPU:1, one launch (start us, length us, event | category | flops | bytes accessed | tf_op | source)
XLA Modules:
  0.0 473.4 jit_solution(16089108275650392793)
XLA Ops:
  8.0 76.3 %all-gather.6.cloned.1.call-done = bf16[1,2048,2048]{2,1,0:T(8,128)(2,1)} async-done(((bf16[1,128,2048]{2,1,0:T(8,128)(2,1)}), bf16[1,2048,2048]{2,1,0:T(8,128)(2,1)}) %all-gather.6.cloned.1.call-update) | async-done | bytes 8388624 | tf_op jit(solution)/shard_map/all_gather | solution.py:60
  84.3 6.9 %fusion.7 = bf16[224,2048]{1,0:T(8,128)(2,1)} fusion(bf16[1,2048,2048]{2,1,0:T(8,128)(2,1)} %all-gather.6.cloned.1.call-done, bf16[1,224,2048]{2,1,0:T(8,128)(2,1)S(1)} %copy-done), kind=kOutput, calls=%fused_computation.16 | convolution fusion | flops 1879506944 | bytes 10223616 | tf_op jit(solution)/shard_map/rp,np->rn/dot_general | solution.py:57
  91.5 46.9 %all_to_all.20 = bf16[16,128,512]{2,1,0:T(8,128)(2,1)S(1)} all-to-all(bf16[16,128,512]{2,1,0:T(8,128)(2,1)S(1)} %broadcast_in_dim.42), channel_id=1, replica_groups=mesh['grp'=8,'hlp'=16] {'hlp'}, dimensions={0} | all-to-all | bytes 4194304 | tf_op jit(solution)/shard_map/all_to_all | solution.py:15
  139.0 3.5 all-to-all-start.1
  143.6 5.3 %all-to-all-done.1 = s32[16,1,224]{2,1,0:T(1,128)S(1)} async-done(((s32[16,1,224]{2,1,0:T(1,128)}), s32[16,1,224]{2,1,0:T(1,128)S(1)}, u32[]{:S(2)}, u32[]{:S(2)}) %all-to-all-start.1) | async-done | bytes 14368 | tf_op jit(solution)/shard_map/all_to_all | solution.py:15
  151.3 3.7 all-to-all-start.2
  158.1 47.0 %all-to-all-done.2 = bf16[16,128,512]{2,1,0:T(8,128)(2,1)S(1)} async-done(((bf16[16,128,512]{2,1,0:T(8,128)(2,1)}), bf16[16,128,512]{2,1,0:T(8,128)(2,1)S(1)}, u32[]{:S(2)}, u32[]{:S(2)}) %all-to-all-start.2) | async-done | bytes 2097184 | tf_op jit(solution)/shard_map/all_to_all | solution.py:15
  206.5 2.5 scatter_custom_fusion.2
  209.3 20.9 %all-gather.4.cloned.1.call-done = bf16[3584,2048]{1,0:T(8,128)(2,1)} async-done(((bf16[224,2048]{1,0:T(8,128)(2,1)}), bf16[3584,2048]{1,0:T(8,128)(2,1)}) %all-gather.4.cloned.1.call-update) | async-done | bytes 14680080 | tf_op jit(solution)/shard_map/all_gather | solution.py:66
  230.2 12.5 %fusion.4 = f32[3584,224]{0,1:T(8,128)} fusion(bf16[224,2048]{1,0:T(8,128)(2,1)} %fusion.7, bf16[3584,2048]{1,0:T(8,128)(2,1)} %all-gather.4.cloned.1.call-done, f32[1,224,3584]{2,1,0:T(8,128)} %param.10), kind=kOutput, calls=%fused_computation.13 | convolution fusion | flops 3289137152 | bytes 22020096 | tf_op jit(solution)/shard_map/rp,np->rn/dot_general | solution.py:63
  242.7 5.0 %copy.14 = f32[3584,224]{1,0:T(8,128)} copy(f32[3584,224]{0,1:T(8,128)} %fusion.4) | data formatting | bytes 6422528 | tf_op jit(solution)/shard_map/sub | solution.py:63
  247.7 19.3 %scatter_custom_fusion = f32[224,7168]{0,1:T(8,128)} fusion(s32[3584]{0:T(1024)S(1)} %fusion.22, f32[3584,224]{1,0:T(8,128)} %copy.14, f32[]{:T(128)} %constant.15.clone.1), kind=kCustom, calls=%fused_computation.14 | custom fusion | bytes 6423040 | tf_op jit(solution)/shard_map/scatter | solution.py:86
  267.0 8.2 %copy.15 = f32[224,7168]{1,0:T(8,128)} copy(f32[224,7168]{0,1:T(8,128)} %scatter_custom_fusion) | data formatting | bytes 12845056 | tf_op jit(solution)/shard_map/scatter | solution.py:86
  275.2 11.1 %scatter_custom_fusion.1 = f32[384,7168]{1,0:T(8,128)} fusion(s32[224]{0:T(256)S(1)} %bitcast.65, f32[224,7168]{1,0:T(8,128)} %copy.15, f32[]{:T(128)} %constant.15.clone.1), kind=kCustom, calls=%fused_computation.10 | custom fusion | bytes 11010560 | tf_op jit(solution)/shard_map/scatter | solution.py:88
  286.3 7.3 %convert_element_type.75 = bf16[384,7168]{1,0:T(8,128)(2,1)} convert(f32[384,7168]{1,0:T(8,128)} %scatter_custom_fusion.1) | non-fusion elementwise | flops 2752512 | bytes 16515072 | tf_op jit(solution)/shard_map/convert_element_type | solution.py:100
  293.6 12.3 %convert_element_type.76 = bf16[128,3,7168]{2,1,0:T(4,128)(2,1)} reshape(bf16[384,7168]{1,0:T(8,128)(2,1)} %convert_element_type.75) | data formatting | bytes 11010048 | tf_op jit(solution)/shard_map/convert_element_type | solution.py:100
  305.8 5.6 %pad_maximum_fusion = bf16[128,3,7681]{2,1,0:T(4,128)(2,1)S(1)} fusion(bf16[128,3,1]{2,1,0:T(4,128)(2,1)S(1)} %convert_element_type.89, bf16[128,3,512]{2,1,0:T(4,128)(2,1)S(1)} %convert_element_type.80, bf16[128,3,7168]{2,1,0:T(4,128)(2,1)} %convert_element_type.76), kind=kLoop, calls=%fused_computation.8 | loop fusion | flops 17697024 | bytes 11798016 | tf_op jit(solution)/shard_map/concatenate | solution.py:24
  311.4 100.1 %all_to_all.21 = bf16[128,3,7681]{2,1,0:T(4,128)(2,1)S(1)} all-to-all(bf16[128,3,7681]{2,1,0:T(4,128)(2,1)S(1)} %pad_maximum_fusion), channel_id=1, replica_groups=mesh['grp'=8,'hlp'=16] {'grp','hlp'}, dimensions={0} | all-to-all | bytes 11798016 | tf_op jit(solution)/shard_map/all_to_all | solution.py:26
  411.5 3.1 copy-done.2
  416.7 9.3 %slice_convert_fusion = f32[128,3,7168]{2,1,0:T(4,128)} fusion(bf16[128,3,7681]{2,1,0:T(4,128)(2,1)} %copy-done.2), kind=kLoop, calls=%fused_computation.9 | loop fusion | flops 2752512 | bytes 16515072 | tf_op jit(solution)/shard_map/reshape | solution.py:111
  426.0 16.5 %reshape.246 = f32[384,7168]{1,0:T(8,128)} reshape(f32[128,3,7168]{2,1,0:T(4,128)} %slice_convert_fusion) | data formatting | bytes 22020096 | tf_op jit(solution)/shard_map/reshape | solution.py:111
  442.4 2.9 scatter_custom_fusion.5
  445.3 17.6 %scatter_custom_fusion.4 = f32[57,7168]{1,0:T(8,128)S(1)} fusion(s32[384]{0:T(512)S(1)} %fusion.23, f32[384,7168]{1,0:T(8,128)} %reshape.246, f32[]{:T(128)} %constant.15.clone.1), kind=kCustom, calls=%fused_computation.21 | custom fusion | flops 2752512 | bytes 1634816 | tf_op jit(solution)/shard_map/scatter-add | solution.py:117
  463.6 2.7 slice_add_fusion
  (54 shorter events, 12.5 us)
Async XLA Ops:
  7.2 77.1 %copy-start = (bf16[1,224,2048]{2,1,0:T(8,128)(2,1)S(1)}, bf16[1,224,2048]{2,1,0:T(8,128)(2,1)}, u32[]{:S(2)}) copy-start(bf16[1,224,2048]{2,1,0:T(8,128)(2,1)} %param.9) | copy-start | bytes 2752516
  7.2 84.1 %copy-start.5 = (bf16[1,128,512]{2,1,0:T(8,128)(2,1)S(1)}, bf16[1,128,512]{2,1,0:T(8,128)(2,1)}, u32[]{:S(2)}) copy-start(bf16[1,128,512]{2,1,0:T(8,128)(2,1)} %param.11) | copy-start | bytes 393220
  7.2 77.1 %all-gather.6.cloned.1.call-start = ((), (), s32[]{:S(2)}) async-start(), calls=%async_computation.5 | async-start | bytes 8912896 | tf_op jit(solution)/shard_map/all_gather | solution.py:60
  7.9 130.4 %copy-start.7 = (s32[1,224]{1,0:T(1,128)S(1)}, s32[1,224]{1,0:T(1,128)}, u32[]{:S(2)}) copy-start(s32[1,224]{1,0:T(1,128)} %param.13) | copy-start | bytes 2692
  7.9 134.5 %copy-start.3 = (bf16[1,128,2048]{2,1,0:T(8,128)(2,1)S(1)}, bf16[1,128,2048]{2,1,0:T(8,128)(2,1)}, u32[]{:S(2)}) copy-start(bf16[1,128,2048]{2,1,0:T(8,128)(2,1)} %param.8) | copy-start | bytes 1572868
  7.9 222.2 %all-gather.4.cloned.1.call-start = ((), (), s32[]{:S(2)}) async-start(), calls=%async_computation.4 | async-start | bytes 15597568 | tf_op jit(solution)/shard_map/all_gather | solution.py:66
  91.5 113.6 %copy-start.4 = (bf16[224,2048]{1,0:T(8,128)(2,1)S(1)}, bf16[224,2048]{1,0:T(8,128)(2,1)}, u32[]{:S(2)}) copy-start(bf16[224,2048]{1,0:T(8,128)(2,1)} %fusion.7) | copy-start | bytes 2752516
  139.0 9.9 %all-to-all-start.1 = ((s32[16,1,224]{2,1,0:T(1,128)}), s32[16,1,224]{2,1,0:T(1,128)S(1)}, u32[]{:S(2)}, u32[]{:S(2)}) async-start(s32[16,1,224]{2,1,0:T(1,128)} %broadcast_in_dim.47), calls=%async_computation.1 | async-start | bytes 32768 | tf_op jit(solution)/shard_map/all_to_all | solution.py:15
  143.6 12.7 %copy-start.8 = (s32[1,224]{1,0:T(1,128)S(1)}, s32[1,224]{1,0:T(1,128)}, u32[]{:S(2)}) copy-start(s32[1,224]{1,0:T(1,128)} %param.13) | copy-start | bytes 2692
  143.6 61.5 %copy-start.9 = (bf16[1,224,512]{2,1,0:T(8,128)(2,1)S(1)}, bf16[1,224,512]{2,1,0:T(8,128)(2,1)}, u32[]{:S(2)}) copy-start(bf16[1,224,512]{2,1,0:T(8,128)(2,1)} %param.12) | copy-start | bytes 688132
  151.3 53.8 %all-to-all-start.2 = ((bf16[16,128,512]{2,1,0:T(8,128)(2,1)}), bf16[16,128,512]{2,1,0:T(8,128)(2,1)S(1)}, u32[]{:S(2)}, u32[]{:S(2)}) async-start(bf16[16,128,512]{2,1,0:T(8,128)(2,1)} %broadcast_in_dim.49), calls=%async_computation.2 | async-start | bytes 4194304 | tf_op jit(solution)/shard_map/all_to_all | solution.py:15
  411.5 3.1 copy-start.2
  426.0 36.9 %copy-start.6 = (f32[56,512]{1,0:T(8,128)S(1)}, f32[56,512]{1,0:T(8,128)}, u32[]{:S(2)}) copy-start(f32[56,512]{1,0:T(8,128)} %param.15) | copy-start | bytes 344068
  426.0 40.3 %copy-start.1 = (bf16[1,224,2048]{2,1,0:T(8,128)(2,1)S(1)}, bf16[1,224,2048]{2,1,0:T(8,128)(2,1)}, u32[]{:S(2)}) copy-start(bf16[1,224,2048]{2,1,0:T(8,128)(2,1)} %param.9) | copy-start | bytes 2752516
Sparse Core Ops, SparseCore 0:
  10.2 74.0 all-gather.5
  91.4 138.7 all-gather.3
where the time goes:
time: 480 us; the launch traced here: 473 us
  waiting for transfers between devices  150 us (31%)
  blocking collectives  147 us (31%)
  local copies, waits for them, and re-layouts  83.7 us (17%)
  other arithmetic  48.7 us (10%)
  matrix products  22 us (5%)
  between operations  14.5 us (3%)
  starting transfers between devices  7.29 us (2%)
    all_to_all x1, blocking collectives, sent_together(): lax.all_to_all(both, axis, split_axis=split_dim, concat_axis=concat_dim,...  100 us
    all_gather x1, waiting for transfers between devices, on_device(): lax.all_gather(inverse, 'hlp', axis=0, tiled=True)  76.3 us
    all_to_all x2, waiting for transfers between devices, sent_to_all(): return lax.all_to_all(copies, axis, split_axis=0, concat_axis=0, tiled=True)  52.3 us
    all_to_all x1, blocking collectives, sent_to_all(): return lax.all_to_all(copies, axis, split_axis=0, concat_axis=0, tiled=True)  46.9 us
    scatter x2, local copies, waits for them, and re-layouts, on_device(): jnp.zeros((local_rows, parent_width), jnp.float32).at[:, full_map]  27.5 us
    all_gather x1, waiting for transfers between devices, on_device(): lax.all_gather(lower_part, 'hlp', axis=0, tiled=True)  20.9 us
    scatter-add x1, other arithmetic, on_device(): jnp.zeros((owned + 1, parent_width), jnp.float32).at[row_index].add(rows_in)  17.6 us
    reshape x1, local copies, waits for them, and re-layouts, on_device(): rows_in = received[0].reshape(devices * capacity, row_width)  16.5 us
  transfers between devices with their start and end apart: 4, of which 4 were waited for; matrix products, arithmetic and copies ran while one was open for 2% of the time, Pallas kernels for 0%

commit v1 on v0

v1 whole, which is shorter than its diff:
```python
import functools

import jax
import jax.numpy as jnp
from jax import lax
from jax.experimental import pallas as pl
from jax.experimental.pallas import tpu as pltpu
from jax.sharding import PartitionSpec as P

MESH = pl.DeviceIdType.MESH
F32, BF16, I32 = jnp.float32, jnp.bfloat16, jnp.int32
NT = (((1,), (1,)), ((), ()))
NN = (((1,), (0,)), ((), ()))


def dot(a, b, dims=NN):
    return lax.dot_general(a, b, dims, preferred_element_type=F32)


def hbm():
    return pl.BlockSpec(memory_space=pl.ANY)


def vmem():
    return pl.BlockSpec(memory_space=pltpu.VMEM)


def onehot(ids, n):
    return (lax.broadcasted_iota(I32, (n, ids.shape[1]), 0) == ids).astype(F32).astype(BF16)


def strict(n):
    r = lax.broadcasted_iota(I32, (n, n), 0)
    c = lax.broadcasted_iota(I32, (n, n), 1)
    return (r < c).astype(F32).astype(BF16)


def joined(parts):
    r = lax.broadcasted_iota(I32, (224, 896), 0)
    c = lax.broadcasted_iota(I32, (224, 896), 1)
    total = jnp.zeros((8, 896), F32)
    for b in range(4):
        shift = (c == r + 224 * b).astype(F32).astype(BF16)
        total = total + dot(parts[b].astype(F32).astype(BF16), shift)
    return total.astype(I32)


def places(member):
    mb = member.astype(BF16)
    before = dot(mb, strict(128))
    count = dot(mb, jnp.ones((128, 128), BF16)).astype(BF16)
    r = lax.broadcasted_iota(I32, (64, 64), 0)
    c = lax.broadcasted_iota(I32, (64, 64), 1)
    above = dot((c < r).astype(F32).astype(BF16), count)
    row_count = dot(jnp.ones((8, 128), BF16), mb, NT).astype(BF16)
    starts = dot(row_count, strict(64))
    return (before + above).astype(I32), starts.astype(I32)


def main_kernel(
    inv, cross, contrib, csrc, psrc, emap,
    arrived, index, start, target, solved_own,
    invf, srcb, low, la, lb, cbuf, sent, held, solved_all, moved, select, slots, outs, mapsb,
    loc_sem, ms, mr, zs, zr, xs, xr, cs, cr, ls, lr, es, er,
):
    g = lax.axis_index("grp")
    h = lax.axis_index("hlp")
    z, x = h // 4, lax.rem(h, 4)
    me = g * 16 + h

    def at(dz, dx):
        return lax.rem(z + dz + 4, 4) * 4 + lax.rem(x + dx + 4, 4)

    def chunks(block):
        return block // 2 + 1

    def each(count, fn, first=0):
        def body(c, carry):
            fn(c)
            return carry

        lax.fori_loop(first, count, body, 0)

    def remote(source, target, ssem, rsem, to):
        return pltpu.make_async_remote_copy(
            source, target, ssem, rsem, device_id={"hlp": to}, device_id_type=MESH
        )

    def wait(ref, sem):
        pltpu.make_async_copy(ref, ref, sem).wait()

    def who(grp, i):
        return lax.rem(grp + g, 8), lax.rem(h + i, 16)

    barrier = pltpu.get_barrier_semaphore()

    def greet(i):
        p = lax.rem(me + i, 128)
        pl.semaphore_signal(barrier, inc=1, device_id=(p // 16, lax.rem(p, 16)), device_id_type=MESH)

    each(128, greet, 1)
    own = pltpu.make_async_copy(inv, invf.at[h], loc_sem.at[0])
    load = pltpu.make_async_copy(contrib, cbuf, loc_sem.at[1])
    load.start()

    def clear(i):
        def chunk(c):
            invf[i, :, pl.ds(pl.multiple_of(c * 256, 256), 256)] = jnp.zeros((128, 256), BF16)

        each(8, chunk, chunks(i))

    each(16, clear)
    own.start()
    mapsb[pl.ds(pl.multiple_of(me * 8, 8), 8), :] = emap[...]
    for b in range(4):
        @pl.when(z == b)
        def _():
            srcb[b, x] = psrc[:, 128 * b : 128 * (b + 1)]

    load.wait()
    for b in range(4):
        sent[b, :, 0:896] = cbuf[:, 896 * b : 896 * (b + 1)].astype(BF16)
        sent[b, :, 896:1024] = csrc[:, 128 * b : 128 * (b + 1)]
    own.wait()
    pl.semaphore_wait(barrier, 127)

    def piece(block, c, part=None):
        cols = pl.ds(pl.multiple_of(c * 256, 256), 256)
        if part is None:
            return invf.at[block, :, cols]
        return invf.at[block, pl.ds(64 * part, 64), cols]

    def map_rows(first, count):
        return mapsb.at[pl.ds(pl.multiple_of(first * 8, 8), count * 8), :]

    def send_z(c):
        remote(piece(h, c), piece(h, c), zs.at[0, c], zr.at[0, c], at(1, 0)).start()
        remote(piece(h, c), piece(h, c), zs.at[1, c], zr.at[1, c], at(-1, 0)).start()

    def send_x(r, block):
        def go(c):
            remote(piece(block, c), piece(block, c), xs.at[r, 0, c], xr.at[r, 0, c], at(0, 1)).start()
            remote(piece(block, c), piece(block, c), xs.at[r, 1, c], xr.at[r, 1, c], at(0, -1)).start()

        return go

    def pass_z(block, d, step):
        def go(c):
            wait(piece(block, c), zr.at[d, c])
            remote(
                piece(block, c, d), piece(block, c, d), zs.at[2 + d, c], zr.at[2 + d, c], at(step, 0)
            ).start()

        return go

    offsets = (0, -1, 1, 2)

    def pass_x(r):
        for d, dx in ((0, -1), (1, 1)):
            block = at(offsets[r], dx)

            def go(c, d=d, dx=dx, block=block):
                wait(piece(block, c), xr.at[r, d, c])
                remote(
                    piece(block, c, d), piece(block, c, d), xs.at[r, 2 + d, c], xr.at[r, 2 + d, c], at(0, -dx)
                ).start()

            each(chunks(block), go)

    for i in (1, 2, 3):
        remote(map_rows(me, 1), map_rows(me, 1), ms.at[0, i], mr.at[0, i], at(0, i)).start()
    each(chunks(h), send_z)
    each(chunks(h), send_x(0, h))
    for i in (1, 2, 3):
        to = lax.rem(z + i, 4)
        cols = pl.ds(pl.multiple_of(to * 128, 128), 128)
        remote(psrc.at[:, cols], srcb.at[z, x], cs.at[0, i], cr.at[0, i], at(i, 0)).start()
    for i in (1, 2, 3):
        wait(map_rows(me, 1), mr.at[0, i])
    line = g * 16 + z * 4
    for i in (1, 2, 3):
        remote(map_rows(line, 4), map_rows(line, 4), ms.at[1, i], mr.at[1, i], at(i, 0)).start()

    def first(c):
        pass_z(at(-1, 0), 0, 1)(c)
        send_x(1, at(-1, 0))(c)

    def second(c):
        pass_z(at(1, 0), 1, -1)(c)
        send_x(2, at(1, 0))(c)

    each(chunks(at(-1, 0)), first)
    each(chunks(at(1, 0)), second)
    for i in (1, 2, 3):
        to = lax.rem(z + i, 4)
        remote(sent.at[to], held.at[z], cs.at[1, i], cr.at[1, i], at(i, 0)).start()
    own_sent = pltpu.make_async_copy(sent.at[z], held.at[z], loc_sem.at[2])
    own_sent.start()
    for i in (1, 2, 3):
        wait(map_rows(line, 4), mr.at[1, i])
    for i in range(1, 8):
        pltpu.make_async_remote_copy(
            map_rows(g * 16, 16), map_rows(g * 16, 16), ms.at[2, i], mr.at[2, i],
            device_id=(lax.rem(g + i, 8), h), device_id_type=MESH,
        ).start()
    pass_x(0)
    for i in (1, 2, 3):
        wait(srcb.at[z, x], cr.at[0, i])
    for i in (1, 2, 3):
        remote(srcb.at[:, x], srcb.at[:, x], cs.at[2, i], cr.at[2, i], at(0, i)).start()

    def third(c):
        wait(piece(at(2, 0), c, 0), zr.at[2, c])
        wait(piece(at(2, 0), c, 1), zr.at[3, c])
        send_x(3, at(2, 0))(c)

    each(chunks(at(2, 0)), third)
    pass_x(1)

    rings = ((la, z, 1, 0), (lb, x, 0, 1))

    def slab(r, dz=0):
        return pl.ds(pl.multiple_of(lax.rem(z + dz + offsets[r] + 4, 4) * 512, 512), 512)

    def lpart(ref, i, part, r, dz=0):
        return ref.at[i, pl.ds(112 * part, 112), slab(r, dz)]

    def factor(r):
        block = at(offsets[r], 2)

        def arrive(c):
            wait(piece(block, c, 0), xr.at[r, 2, c])
            wait(piece(block, c, 1), xr.at[r, 3, c])

        each(chunks(block), arrive)
        zz = lax.rem(z + offsets[r] + 4, 4)
        for part in range(2):
            m = 2 * zz + part
            rows = invf[pl.ds(2 * m, 2)].reshape(256, 2048)
            low[:, pl.ds(pl.multiple_of(m * 256, 256), 256)] = dot(cross[...], rows, NT).astype(BF16)
        for order in (0, 1):
            for a, (ref, mine, dz, dx) in enumerate(rings):
                for d, step in ((0, 1), (1, -1)):
                    part = order if d == 0 else 1 - order
                    remote(
                        low.at[pl.ds(112 * part, 112), slab(r)], lpart(ref, mine, part, r),
                        ls.at[a, d, part, r], lr.at[a, d, part, r], at(dz * step, dx * step),
                    ).start()

    def factor_pass(r):
        for a, (ref, mine, dz, dx) in enumerate(rings):
            for d, step in ((0, 1), (1, -1)):
                block = lax.rem(mine - step + 4, 4)
                part = lpart(ref, block, d, r, -dz * step)
                wait(part, lr.at[a, d, d, r])
                remote(part, part, ls.at[a, 2, d, r], lr.at[a, 2, d, r], at(dz * step, dx * step)).start()

    factor(0)
    pass_x(2)
    factor(1)
    factor_pass(0)
    pass_x(3)

    own_maps = [mapsb[pl.ds(pl.multiple_of((line + b) * 8, 8), 8), :] for b in range(4)]
    high = onehot(joined([v // 128 for v in own_maps])[0:1], 64)
    lows = onehot(joined([lax.rem(v, 128) for v in own_maps])[0:1], 128)
    place, _ = places(dot(high, lows, NT))
    rank = jnp.zeros((1, 896), I32)
    for value, scale in ((place // 128, 128), (lax.rem(place, 128), 1)):
        found = dot(value.astype(F32).astype(BF16), lows) * high.astype(F32)
        rank = rank + jnp.sum(found, axis=0, keepdims=True).astype(I32) * scale
    select[...] = onehot(rank, 896)

    owners, slot_ids = [], []
    for k in range(4):
        owner = mapsb[pl.ds(pl.multiple_of((g * 16 + 4 * k + x) * 8, 8), 8), :] // 56
        hot = onehot(owner[0:1], 128)
        earlier = dot(hot, strict(224)) * hot.astype(F32)
        pos = jnp.sum(earlier, axis=0, keepdims=True).astype(I32)
        owners.append(owner)
        slot_ids.append(jnp.broadcast_to(pos + 3 * k, (8, 224)))
    owner, slot = joined(owners)[0:1], joined(slot_ids)[0:1]
    slots[0:1] = owner * 16 + slot
    for q in range(3):
        slots[q + 1 : q + 2] = jnp.where(slot // 4 == q, owner * 16 + 12 + lax.rem(slot, 4), -1)

    factor(2)
    factor_pass(1)
    for i in (1, 2, 3):
        wait(srcb.at[:, x], cr.at[2, i])
    factor(3)
    factor_pass(2)
    sources = srcb[...].reshape(2048, 128)

    def solve(m):
        rows = invf[pl.ds(2 * m, 2)].reshape(256, 2048)
        solved_all[pl.ds(pl.multiple_of(m * 256, 256), 256), :] = dot(rows, sources).astype(BF16)

    each(8, solve)
    for i in (1, 2, 3):
        to = at(i, 0)
        remote(
            solved_all.at[pl.ds(pl.multiple_of(to * 128, 128), 128), :], solved_own.at[z],
            cs.at[3, i], cr.at[3, i], to,
        ).start()
    own_s = pltpu.make_async_copy(
        solved_all.at[pl.ds(pl.multiple_of(h * 128, 128), 128), :], solved_own.at[z], loc_sem.at[3]
    )
    own_s.start()
    la[z] = low[...]
    lb[x] = low[...]
    factor_pass(3)
    for i in (1, 2, 3):
        wait(held.at[z], cr.at[1, i])
    own_sent.wait()
    for r in range(4):
        for a, (ref, mine, dz, dx) in enumerate(rings):
            for d, step in ((0, 1), (1, -1)):
                block = lax.rem(mine - step + 4, 4)
                wait(lpart(ref, block, 1 - d, r, -dz * step), lr.at[a, d, 1 - d, r])
                wait(lpart(ref, lax.rem(mine + 2, 4), d, r, 2 * dz), lr.at[a, 2, d, r])

    def rows_of(k):
        left = la[k]
        got = (held[k, :, 0:896].astype(F32) - dot(left, lb[...].reshape(896, 2048), NT)).astype(BF16)
        moved[k, :, 0:896] = dot(got, select[...], NT).astype(BF16)
        moved[k, :, 896:1024] = (held[k, :, 896:1024].astype(F32) - dot(left, solved_all[...])).astype(BF16)

    each(4, rows_of)

    def send_rows(j):
        grp = lax.rem(g + j, 8)
        row = lax.broadcasted_iota(I32, (256, 896), 0) + grp * 256
        main = (row == slots[0:1]).astype(F32).astype(BF16)
        last = moved[:, :, 768:1024].reshape(896, 256)
        for q in range(3):
            extra = (row == slots[q + 1 : q + 2]).astype(F32).astype(BF16)
            part = dot(main, moved[:, :, 256 * q : 256 * (q + 1)].reshape(896, 256)) + dot(extra, last)
            outs[pl.ds(grp * 16, 16), :, 256 * q : 256 * (q + 1)] = part.astype(BF16).reshape(16, 16, 256)

        def go(i):
            to = lax.rem(h + i, 16)

            @pl.when((j != 0) | (i != 0))
            def _():
                pltpu.make_async_remote_copy(
                    outs.at[grp * 16 + to], arrived.at[me], es, er, device_id=(grp, to), device_id_type=MESH
                ).start()

        each(16, go)

    each(8, send_rows)
    own_rows = pltpu.make_async_copy(outs.at[me], arrived.at[me], loc_sem.at[4])
    own_rows.start()

    for i in range(1, 8):
        wait(map_rows(0, 16), mr.at[2, i])

    def table(i):
        member = jnp.zeros((64, 128), F32)
        for b in range(4):
            v = mapsb[pl.ds(pl.multiple_of((4 * i + b) * 8, 8), 8), :][0:1]
            member = member + dot(onehot(v // 128, 64), onehot(lax.rem(v, 128), 128), NT)
        place, starts = places(member)
        index[i] = jnp.where(member > 0.5, lax.rem(place, 128), -1)[:56]
        start[i] = jnp.minimum(starts, 895)

    each(32, table)
    every = mapsb[...]
    r = lax.broadcasted_iota(I32, (128, 1024), 0)
    c = lax.broadcasted_iota(I32, (128, 1024), 1)
    eighth = (c == 8 * r).astype(F32).astype(BF16)
    mine = (every // 56 == me).astype(F32)
    local = dot(eighth, ((lax.rem(every, 56) + 1).astype(F32) * mine).astype(BF16))
    mine = dot(eighth, mine.astype(BF16))
    pos = dot(mine.astype(BF16), strict(224))
    r = lax.broadcasted_iota(I32, (128, 64), 0)
    c = lax.broadcasted_iota(I32, (128, 64), 1)
    keep = lax.broadcasted_iota(I32, (8, 128), 1) // 16 == lax.broadcasted_iota(I32, (8, 128), 0)
    totals = [jnp.zeros((8, 64), F32) for _ in range(4)]
    for p in range(3):
        found = jnp.where(pos == p, local, 0.0).astype(BF16)
        line_of = dot(jnp.ones((8, 224), BF16), found, NT)
        line_of = jnp.where(keep, line_of, 0.0).astype(BF16)
        slot_of = 3 * lax.rem(r // 4, 4) + p
        for v in range(4):
            want = slot_of if v == 0 else slot_of - 4 * (v - 1) + 12
            fits = (lax.rem(r, 4) == c // 16) & (want == lax.rem(c, 16))
            if v > 0:
                fits = fits & (lax.rem(c, 16) >= 12)
            totals[v] = totals[v] + dot(line_of, fits.astype(F32).astype(BF16))
    for v in range(4):
        target[v] = totals[v].astype(I32) - 1

    def sent_z(c):
        for d in (0, 1):
            wait(piece(h, c), zs.at[d, c])

    each(chunks(h), sent_z)
    for d, dz in ((0, -1), (1, 1)):

        def sent_pass(c, d=d, dz=dz):
            wait(piece(at(dz, 0), c, d), zs.at[2 + d, c])

        each(chunks(at(dz, 0)), sent_pass)
    for r in range(4):

        def sent_x(c, r=r):
            for d in (0, 1):
                wait(piece(at(offsets[r], 0), c), xs.at[r, d, c])

        each(chunks(at(offsets[r], 0)), sent_x)
        for d, dx in ((0, -1), (1, 1)):

            def sent_pass_x(c, r=r, d=d, dx=dx):
                wait(piece(at(offsets[r], dx), c, d), xs.at[r, 2 + d, c])

            each(chunks(at(offsets[r], dx)), sent_pass_x)
    for i in (1, 2, 3):
        wait(map_rows(me, 1), ms.at[0, i])
        wait(map_rows(line, 4), ms.at[1, i])
        wait(srcb.at[z, x], cs.at[0, i])
        wait(held.at[z], cs.at[1, i])
        wait(srcb.at[:, x], cs.at[2, i])
        wait(solved_own.at[z], cs.at[3, i])
        wait(solved_own.at[z], cr.at[3, i])
    for i in range(1, 8):
        wait(map_rows(0, 16), ms.at[2, i])
    for r in range(4):
        for a, (ref, mine_at, dz, dx) in enumerate(rings):
            for d in (0, 1):
                for part in (0, 1):
                    wait(lpart(ref, mine_at, part, r), ls.at[a, d, part, r])
                wait(lpart(ref, mine_at, d, r), ls.at[a, 2, d, r])
    own_s.wait()
    own_rows.wait()
    some = pl.ds(0, 127)
    wait(outs.at[some], es)
    wait(arrived.at[some], er)


def main_call(inv, cross, contrib, csrc, psrc, emap):
    dma = pltpu.SemaphoreType.DMA
    return pl.pallas_call(
        main_kernel,
        out_shape=(
            jax.ShapeDtypeStruct((128, 16, 768), BF16),
            jax.ShapeDtypeStruct((32, 56, 128), I32),
            jax.ShapeDtypeStruct((32, 8, 64), I32),
            jax.ShapeDtypeStruct((4, 8, 64), I32),
            jax.ShapeDtypeStruct((4, 128, 128), BF16),
        ),
        in_specs=[hbm(), vmem(), hbm(), vmem(), vmem(), vmem()],
        out_specs=(hbm(), vmem(), vmem(), vmem(), hbm()),
        scratch_shapes=[
            pltpu.VMEM((16, 128, 2048), BF16),
            pltpu.VMEM((4, 4, 128, 128), BF16),
            pltpu.VMEM((224, 2048), BF16),
            pltpu.VMEM((4, 224, 2048), BF16),
            pltpu.VMEM((4, 224, 2048), BF16),
            pltpu.VMEM((224, 3584), F32),
            pltpu.VMEM((4, 224, 1024), BF16),
            pltpu.VMEM((4, 224, 1024), BF16),
            pltpu.VMEM((2048, 128), BF16),
            pltpu.VMEM((4, 224, 1024), BF16),
            pltpu.VMEM((896, 896), BF16),
            pltpu.VMEM((8, 896), I32),
            pltpu.VMEM((128, 16, 768), BF16),
            pltpu.VMEM((1024, 224), I32),
            dma((5,)),
            dma((3, 8)), dma((3, 8)),
            dma((4, 8)), dma((4, 8)),
            dma((4, 4, 8)), dma((4, 4, 8)),
            dma((4, 4)), dma((4, 4)),
            dma((2, 3, 2, 4)), dma((2, 3, 2, 4)),
            dma, dma,
        ],
        compiler_params=pltpu.CompilerParams(
            collective_id=0, has_side_effects=True, vmem_limit_bytes=56 << 20
        ),
        name="fronts",
    )(inv, cross, contrib, csrc, psrc, emap)


def spread_kernel(start, target, index, rows, parent, rhs, front, right, tile):
    i = pl.program_id(0)

    @pl.when(i == 0)
    def _():
        front[...] = parent[...]
        right[...] = rhs[...]

    row = lax.broadcasted_iota(I32, (56, 64), 0)
    pick = [(row == target[v, 0]).astype(F32).astype(BF16) for v in range(4)]
    tail = jnp.zeros((56, 256), F32)
    for q in range(3):
        got = rows[0, :, 256 * q : 256 * (q + 1)]
        main = dot(pick[0], got)
        tile[2 * q] = main[:, :128]
        tile[2 * q + 1] = main[:, 128:]
        tail = tail + dot(pick[q + 1], got)
    tile[6] = tail[:, :128]
    tile[7] = tail[:, 128:]
    which = lax.rem(i, 4)
    for zz in range(4):

        @pl.when(which == zz)
        def _():
            right[:, 128 * zz : 128 * (zz + 1)] += tail[:, 128:]

    lane = lax.broadcasted_iota(I32, (56, 128), 1)
    for t in range(56):
        at = start[i, t]
        j = at // 128
        both = jnp.where(lane >= lax.rem(at, 128), tile[j], tile[j + 1])
        where = jnp.broadcast_to(index[0, t : t + 1], (56, 128))
        taken = jnp.take_along_axis(both, where & 127, axis=1)
        front[:, 128 * t : 128 * (t + 1)] += jnp.where(where >= 0, taken, 0.0)


def spread(start, target, index, rows, parent, rhs):
    whole = lambda shape: pl.BlockSpec(shape, lambda i: (0,) * len(shape))
    return pl.pallas_call(
        spread_kernel,
        grid=(32,),
        out_shape=(
            jax.ShapeDtypeStruct((56, 7168), F32),
            jax.ShapeDtypeStruct((56, 512), F32),
        ),
        in_specs=[
            pl.BlockSpec(memory_space=pltpu.SMEM),
            pl.BlockSpec((4, 1, 1, 64), lambda i: (0, i // 4, 0, 0)),
            pl.BlockSpec((1, 56, 128), lambda i: (i, 0, 0)),
            pl.BlockSpec((1, 64, 768), lambda i: (i, 0, 0)),
            whole((56, 7168)),
            whole((56, 512)),
        ],
        out_specs=(whole((56, 7168)), whole((56, 512))),
        scratch_shapes=[pltpu.VMEM((8, 56, 128), F32)],
        compiler_params=pltpu.CompilerParams(vmem_limit_bytes=40 << 20),
        name="spread",
    )(start, target, index, rows, parent, rhs)


def on_device(
    pivot_inverse, cross_block, contrib_block, pivot_sources, contrib_sources, ext_map, parent_front, parent_rhs
):
    emap = jnp.broadcast_to(ext_map, (8, 224))
    arrived, index, start, target, solved_own = main_call(
        pivot_inverse[0], cross_block[0], contrib_block[0], contrib_sources[0], pivot_sources[0], emap
    )
    solved = solved_own.transpose(1, 0, 2).reshape(1, 128, 512)
    front, right = spread(
        start[:, 0, :], target.reshape(4, 8, 1, 64), index, arrived.reshape(32, 64, 768), parent_front, parent_rhs
    )
    return solved, front, right


def solution(mesh):
    return jax.shard_map(
        on_device,
        mesh=mesh,
        in_specs=(
            P("grp", "hlp", None),
            P("grp", "hlp", None),
            P("grp", "hlp", None),
            P("grp", "hlp", None),
            P("grp", "hlp", None),
            P("grp", "hlp"),
            P(("grp", "hlp"), None),
            P(("grp", "hlp"), None),
        ),
        out_specs=(P("grp", "hlp", None), P(("grp", "hlp"), None), P(("grp", "hlp"), None)),
        check_vma=False,
    )
```

time: 480 us -> 188 us (0.39); the launches traced: 473 us -> 188 us
  Pallas kernels: 0 us -> 179 us
  waiting for transfers between devices: 150 us -> 0 us
  blocking collectives: 147 us -> 0 us
  local copies, waits for them, and re-layouts: 83.7 us -> 7.92 us
  other arithmetic: 48.7 us -> 0 us
  matrix products: 22 us -> 0 us
  between operations: 14.5 us -> 0.7 us
  starting transfers between devices: 7.29 us -> 0 us
    pallas_call x0 -> x2, Pallas kernels: none -> 179 us  [the longest x1 147 us: main_call(): pl.pallas_call(main_kernel, out_shape=(jax.ShapeDtypeStruct((128, 16, 768...]
    all_to_all x2 -> x0, blocking collectives: 147 us -> none  [the longest x1 100 us: sent_together(): lax.all_to_all(both, axis, split_axis=split_dim, concat_axis=concat_dim,...]
    all_gather x2 -> x0, waiting for transfers between devices: 97.2 us -> none  [the longest x1 76.3 us: on_device(): lax.all_gather(inverse, 'hlp', axis=0, tiled=True)]
    all_to_all x2 -> x0, waiting for transfers between devices: 52.3 us -> none  [sent_to_all(): return lax.all_to_all(copies, axis, split_axis=0, concat_axis=0, tiled=True)]
    scatter x5 -> x0, local copies, waits for them, and re-layouts: 42.4 us -> none  [the longest x2 27.5 us: on_device(): jnp.zeros((local_rows, parent_width), jnp.float32).at[:, full_map]]
    dot_general x4 -> x0, matrix products: 22 us -> none  [the longest x1 12.5 us: on_device(): jnp.einsum('rp,np->rn', lower_part, lax.all_gather(lower_part, 'hlp', axi...]
    scatter-add x2 -> x0, other arithmetic: 20.4 us -> none  [the longest x1 17.6 us: on_device(): jnp.zeros((owned + 1, parent_width), jnp.float32).at[row_index].add(rows_in)]
    reshape x2 -> x0, local copies, waits for them, and re-layouts: 16.9 us -> none  [the longest x1 16.5 us: on_device(): rows_in = received[0].reshape(devices * capacity, row_width)]
  transfers between devices with their start and end apart: 4 -> 0, of which waited for: 4 -> 0; matrix products, arithmetic and copies ran while one was open for 2% -> 0% of each run, Pallas kernels for 0% -> 0%
where the time goes in v1:
time: 188 us
  Pallas kernels  179 us (95%)
  local copies, waits for them, and re-layouts  7.92 us (4%)
    pallas_call x1, Pallas kernels, main_call(): pl.pallas_call(main_kernel, out_shape=(jax.ShapeDtypeStruct((128, 16, 768...  147 us
    pallas_call x1, Pallas kernels, spread(): pl.pallas_call(spread_kernel, grid=(32,), out_shape=(jax.ShapeDtypeStruct...  31.9 us
    unnamed x11, local copies, waits for them, and re-layouts  4.56 us

profile of v1, /device:TPU:1, one launch (start us, length us, event | category | flops | bytes accessed | tf_op | source)
XLA Modules:
  0.0 187.7 jit_solution(14319885846233848132)
XLA Ops:
  0.6 0.0 copy-start.3
  0.6 0.0 copy-start.1
  0.7 1.4 broadcast_in_dim.8.emap
  2.1 147.2 %fronts.1 = (bf16[128,16,768]{2,1,0:T(8,128)(2,1)}, s32[32,56,128]{2,1,0:T(8,128)}, s32[32,8,64]{2,1,0:T(8,128)}, s32[4,8,64]{2,1,0:T(8,128)}, bf16[4,128,128]{2,1,0:T(8,128)(2,1)}) custom-call(bf16[128,2048]{1,0:T(8,128)(2,1)} %bitcast.16, bf16[224,2048]{1,0:T(8,128)(2,1)} %bitcast.15, f32[224,3584]{1,0:T(8,128)} %bitcast.14, bf16[224,512]{1,0:T(8,128)(2,1)} %bitcast.18, ...), custom_call_target="tpu_custom_call" | custom-call | tf_op jit(solution)/shard_map/fronts/pallas_call | solution.py:444
  149.3 1.0 copy.12
  150.3 0.8 copy.14
  151.1 0.9 copy.13
  152.0 0.0 copy-done.3
  152.0 0.0 copy-done.1
  152.0 0.0 copy-start
  152.0 1.9 %copy-done = bf16[128,16,768]{2,1,0:T(8,128)(2,1)S(1)} copy-done((bf16[128,16,768]{2,1,0:T(8,128)(2,1)S(1)}, bf16[128,16,768]{2,1,0:T(8,128)(2,1)}, u32[]{:S(2)}) %copy-start) | copy-done | bytes 3145752
  153.9 0.0 copy-start.2
  153.9 1.2 copy-done.2
  155.1 0.0 copy-start.4
  155.1 0.7 copy-done.4
  155.8 31.9 %spread.1 = (f32[56,7168]{1,0:T(8,128)}, f32[56,512]{1,0:T(8,128)}) custom-call(s32[32,64]{1,0:T(8,128)S(1)} %slice_bitcast_fusion.start, s32[4,8,1,64]{3,2,1,0:T(1,128)S(1)} %bitcast.13, s32[32,56,128]{2,1,0:T(8,128)S(1)} %copy-done.2, bf16[32,64,768]{2,1,0:T(8,128)(2,1)S(1)} %bitcast.12, f32[56,7168]{1,0:T(8,128)S(1)} %copy-done.1, f32[56,512]{1,0:T(8,128)S(1)} %copy-done.3), custom_call_target="tpu_custom_call" | custom-call | tf_op jit(solution)/shard_map/spread/pallas_call | solution.py:523
  (1 shorter events, 0.0 us)
Async XLA Ops:
  0.6 151.4 %copy-start.3 = (f32[56,512]{1,0:T(8,128)S(1)}, f32[56,512]{1,0:T(8,128)}, u32[]{:S(2)}) copy-start(f32[56,512]{1,0:T(8,128)} %rhs.1) | copy-start | bytes 344068
  0.6 151.4 %copy-start.1 = (f32[56,7168]{1,0:T(8,128)S(1)}, f32[56,7168]{1,0:T(8,128)}, u32[]{:S(2)}) copy-start(f32[56,7168]{1,0:T(8,128)} %parent.1) | copy-start | bytes 4816900
  152.0 1.9 %copy-start = (bf16[128,16,768]{2,1,0:T(8,128)(2,1)S(1)}, bf16[128,16,768]{2,1,0:T(8,128)(2,1)}, u32[]{:S(2)}) copy-start(bf16[128,16,768]{2,1,0:T(8,128)(2,1)} %get-tuple-element.14) | copy-start | bytes 9437188
  153.9 1.2 copy-start.2
  155.1 0.7 copy-start.4

commit v2 on v1

--- a/solution.py
+++ b/solution.py
@@ -11,6 +11,7 @@
 F32, BF16, I32 = jnp.float32, jnp.bfloat16, jnp.int32
 NT = (((1,), (1,)), ((), ()))
 NN = (((1,), (0,)), ((), ()))
+UNROLL = 8
 
 
 def dot(a, b, dims=NN):
@@ -27,6 +28,10 @@
 
 def onehot(ids, n):
     return (lax.broadcasted_iota(I32, (n, ids.shape[1]), 0) == ids).astype(F32).astype(BF16)
+
+
+def onehot_rows(ids):
+    return (lax.broadcasted_iota(I32, (56, ids.shape[1]), 0) == ids).astype(F32).astype(BF16)
 
 
 def strict(n):
@@ -58,9 +63,10 @@
 
 
 def main_kernel(
-    inv, cross, contrib, csrc, psrc, emap,
-    arrived, index, start, target, solved_own,
+    inv, cross, contrib, csrc, psrc, emap, parent, rhs,
+    front, right, solved_own,
     invf, srcb, low, la, lb, cbuf, sent, held, solved_all, moved, select, slots, outs, mapsb,
+    arrived, index, start, start_at, target, tile,
     loc_sem, ms, mr, zs, zr, xs, xr, cs, cr, ls, lr, es, er,
 ):
     g = lax.axis_index("grp")
@@ -102,6 +108,12 @@
     own = pltpu.make_async_copy(inv, invf.at[h], loc_sem.at[0])
     load = pltpu.make_async_copy(contrib, cbuf, loc_sem.at[1])
     load.start()
+    base = (
+        pltpu.make_async_copy(parent, front, loc_sem.at[5]),
+        pltpu.make_async_copy(rhs, right, loc_sem.at[6]),
+    )
+    for copy in base:
+        copy.start()
 
     def clear(i):
         def chunk(c):
@@ -255,10 +267,23 @@
                 wait(part, lr.at[a, d, d, r])
                 remote(part, part, ls.at[a, 2, d, r], lr.at[a, 2, d, r], at(dz * step, dx * step)).start()
 
+    def table(i):
+        member = jnp.zeros((64, 128), F32)
+        for b in range(4):
+            v = mapsb[pl.ds(pl.multiple_of((4 * i + b) * 8, 8), 8), :][0:1]
+            member = member + dot(onehot(v // 128, 64), onehot(lax.rem(v, 128), 128), NT)
+        place, starts = places(member)
+        index[i] = jnp.where(member > 0.5, lax.rem(place, 128), -1)[:56]
+        start[i] = jnp.clip(starts, 0, 895)
+
     factor(0)
+    for i in range(1, 8):
+        wait(map_rows(0, 16), mr.at[2, i])
+    each(8, table)
     pass_x(2)
     factor(1)
     factor_pass(0)
+    each(16, table, 8)
     pass_x(3)
 
     own_maps = [mapsb[pl.ds(pl.multiple_of((line + b) * 8, 8), 8), :] for b in range(4)]
@@ -286,6 +311,7 @@
 
     factor(2)
     factor_pass(1)
+    each(24, table, 16)
     for i in (1, 2, 3):
         wait(srcb.at[:, x], cr.at[2, i])
     factor(3)
@@ -309,63 +335,10 @@
     own_s.start()
     la[z] = low[...]
     lb[x] = low[...]
-    factor_pass(3)
-    for i in (1, 2, 3):
-        wait(held.at[z], cr.at[1, i])
-    own_sent.wait()
-    for r in range(4):
-        for a, (ref, mine, dz, dx) in enumerate(rings):
-            for d, step in ((0, 1), (1, -1)):
-                block = lax.rem(mine - step + 4, 4)
-                wait(lpart(ref, block, 1 - d, r, -dz * step), lr.at[a, d, 1 - d, r])
-                wait(lpart(ref, lax.rem(mine + 2, 4), d, r, 2 * dz), lr.at[a, 2, d, r])
-
-    def rows_of(k):
-        left = la[k]
-        got = (held[k, :, 0:896].astype(F32) - dot(left, lb[...].reshape(896, 2048), NT)).astype(BF16)
-        moved[k, :, 0:896] = dot(got, select[...], NT).astype(BF16)
-        moved[k, :, 896:1024] = (held[k, :, 896:1024].astype(F32) - dot(left, solved_all[...])).astype(BF16)
-
-    each(4, rows_of)
-
-    def send_rows(j):
-        grp = lax.rem(g + j, 8)
-        row = lax.broadcasted_iota(I32, (256, 896), 0) + grp * 256
-        main = (row == slots[0:1]).astype(F32).astype(BF16)
-        last = moved[:, :, 768:1024].reshape(896, 256)
-        for q in range(3):
-            extra = (row == slots[q + 1 : q + 2]).astype(F32).astype(BF16)
-            part = dot(main, moved[:, :, 256 * q : 256 * (q + 1)].reshape(896, 256)) + dot(extra, last)
-            outs[pl.ds(grp * 16, 16), :, 256 * q : 256 * (q + 1)] = part.astype(BF16).reshape(16, 16, 256)
-
-        def go(i):
-            to = lax.rem(h + i, 16)
-
-            @pl.when((j != 0) | (i != 0))
-            def _():
-                pltpu.make_async_remote_copy(
-                    outs.at[grp * 16 + to], arrived.at[me], es, er, device_id=(grp, to), device_id_type=MESH
-                ).start()
-
-        each(16, go)
-
-    each(8, send_rows)
-    own_rows = pltpu.make_async_copy(outs.at[me], arrived.at[me], loc_sem.at[4])
-    own_rows.start()
-
-    for i in range(1, 8):
-        wait(map_rows(0, 16), mr.at[2, i])
-
-    def table(i):
-        member = jnp.zeros((64, 128), F32)
-        for b in range(4):
-            v = mapsb[pl.ds(pl.multiple_of((4 * i + b) * 8, 8), 8), :][0:1]
-            member = member + dot(onehot(v // 128, 64), onehot(lax.rem(v, 128), 128), NT)
-        place, starts = places(member)
-        index[i] = jnp.where(member > 0.5, lax.rem(place, 128), -1)[:56]
-        start[i] = jnp.minimum(starts, 895)
-
-    each(32, table)
+    each(32, table, 24)
+    starts_in = pltpu.make_async_copy(start, start_at, loc_sem.at[7])
+    starts_in.start()
+
     every = mapsb[...]
     r = lax.broadcasted_iota(I32, (128, 1024), 0)
     c = lax.broadcasted_iota(I32, (128, 1024), 1)
@@ -392,6 +365,89 @@
     for v in range(4):
         target[v] = totals[v].astype(I32) - 1
 
+    factor_pass(3)
+    for i in (1, 2, 3):
+        wait(held.at[z], cr.at[1, i])
+    own_sent.wait()
+    for r in range(4):
+        for a, (ref, mine, dz, dx) in enumerate(rings):
+            for d, step in ((0, 1), (1, -1)):
+                block = lax.rem(mine - step + 4, 4)
+                wait(lpart(ref, block, 1 - d, r, -dz * step), lr.at[a, d, 1 - d, r])
+                wait(lpart(ref, lax.rem(mine + 2, 4), d, r, 2 * dz), lr.at[a, 2, d, r])
+
+    def rows_of(k):
+        left = la[k]
+        got = (held[k, :, 0:896].astype(F32) - dot(left, lb[...].reshape(896, 2048), NT)).astype(BF16)
+        moved[k, :, 0:896] = dot(got, select[...], NT).astype(BF16)
+        moved[k, :, 896:1024] = (held[k, :, 896:1024].astype(F32) - dot(left, solved_all[...])).astype(BF16)
+
+    each(4, rows_of)
+
+    def send_rows(j, first=0):
+        grp = lax.rem(g + j, 8)
+        row = lax.broadcasted_iota(I32, (256, 896), 0) + grp * 256
+        main = (row == slots[0:1]).astype(F32).astype(BF16)
+        last = moved[:, :, 768:1024].reshape(896, 256)
+        for q in range(3):
+            extra = (row == slots[q + 1 : q + 2]).astype(F32).astype(BF16)
+            part = dot(main, moved[:, :, 256 * q : 256 * (q + 1)].reshape(896, 256)) + dot(extra, last)
+            outs[pl.ds(grp * 16, 16), :, 256 * q : 256 * (q + 1)] = part.astype(BF16).reshape(16, 16, 256)
+
+        def go(i):
+            to = lax.rem(h + i, 16)
+
+            pltpu.make_async_remote_copy(
+                outs.at[grp * 16 + to], arrived.at[me], es, er.at[g], device_id=(grp, to), device_id_type=MESH
+            ).start()
+
+        each(16, go, first)
+
+    send_rows(0, 1)
+    own_rows = pltpu.make_async_copy(outs.at[me], arrived.at[me], er.at[g])
+    own_rows.start()
+    each(8, send_rows, 1)
+
+
+    starts_in.wait()
+    for copy in base:
+        copy.wait()
+
+    def spread(j):
+        grp = lax.rem(g + 8 - j, 8)
+        wait(arrived.at[pl.ds(grp * 16, 16)], er.at[grp])
+        pick = [onehot_rows(target[v, pl.ds(grp, 1), :]) for v in range(4)]
+        for b in range(4):
+            got = arrived[pl.ds(grp * 16 + 4 * b, 4)].reshape(64, 768)
+            tail = jnp.zeros((56, 256), F32)
+            for q in range(3):
+                part = dot(pick[0], got[:, 256 * q : 256 * (q + 1)])
+                tile[b, 2 * q] = part[:, :128]
+                tile[b, 2 * q + 1] = part[:, 128:]
+                tail = tail + dot(pick[q + 1], got[:, 256 * q : 256 * (q + 1)])
+            tile[b, 6] = tail[:, :128]
+            tile[b, 7] = tail[:, 128:]
+            right[:, 128 * b : 128 * (b + 1)] += tail[:, 128:]
+        lane = lax.broadcasted_iota(I32, (56, 128), 1)
+
+        def columns(s):
+            for u in range(UNROLL):
+                t = s * UNROLL + u
+                cols = pl.ds(pl.multiple_of(t * 128, 128), 128)
+                total = front[:, cols]
+                for b in range(4):
+                    begin = start_at[grp * 4 + b, 0, t]
+                    i = jnp.clip(begin // 128, 0, 6)
+                    both = jnp.where(lane >= lax.rem(begin, 128), tile[b, i], tile[b, i + 1])
+                    where = jnp.broadcast_to(index[grp * 4 + b, pl.ds(t, 1), :], (56, 128))
+                    taken = jnp.take_along_axis(both, where & 127, axis=1)
+                    total = total + jnp.where(where >= 0, taken, 0.0)
+                front[:, cols] = total
+
+        each(56 // UNROLL, columns)
+
+    each(8, spread)
+
     def sent_z(c):
         for d in (0, 1):
             wait(piece(h, c), zs.at[d, c])
@@ -433,25 +489,20 @@
                     wait(lpart(ref, mine_at, part, r), ls.at[a, d, part, r])
                 wait(lpart(ref, mine_at, d, r), ls.at[a, 2, d, r])
     own_s.wait()
-    own_rows.wait()
-    some = pl.ds(0, 127)
-    wait(outs.at[some], es)
-    wait(arrived.at[some], er)
-
-
-def main_call(inv, cross, contrib, csrc, psrc, emap):
+    wait(outs.at[pl.ds(0, 127)], es)
+
+
+def main_call(inv, cross, contrib, csrc, psrc, emap, parent, rhs):
     dma = pltpu.SemaphoreType.DMA
     return pl.pallas_call(
         main_kernel,
         out_shape=(
-            jax.ShapeDtypeStruct((128, 16, 768), BF16),
-            jax.ShapeDtypeStruct((32, 56, 128), I32),
-            jax.ShapeDtypeStruct((32, 8, 64), I32),
-            jax.ShapeDtypeStruct((4, 8, 64), I32),
+            jax.ShapeDtypeStruct((56, 7168), F32),
+            jax.ShapeDtypeStruct((56, 512), F32),
             jax.ShapeDtypeStruct((4, 128, 128), BF16),
         ),
-        in_specs=[hbm(), vmem(), hbm(), vmem(), vmem(), vmem()],
-        out_specs=(hbm(), vmem(), vmem(), vmem(), hbm()),
+        in_specs=[hbm(), vmem(), hbm(), vmem(), vmem(), vmem(), hbm(), hbm()],
+        out_specs=(vmem(), vmem(), hbm()),
         scratch_shapes=[
             pltpu.VMEM((16, 128, 2048), BF16),
             pltpu.VMEM((4, 4, 128, 128), BF16),
@@ -467,93 +518,35 @@
             pltpu.VMEM((8, 896), I32),
             pltpu.VMEM((128, 16, 768), BF16),
             pltpu.VMEM((1024, 224), I32),
-            dma((5,)),
+            pltpu.VMEM((128, 16, 768), BF16),
+            pltpu.VMEM((32, 56, 128), I32),
+            pltpu.VMEM((32, 8, 64), I32),
+            pltpu.SMEM((32, 8, 64), I32),
+            pltpu.VMEM((4, 8, 64), I32),
+            pltpu.VMEM((4, 8, 56, 128), F32),
+            dma((8,)),
             dma((3, 8)), dma((3, 8)),
             dma((4, 8)), dma((4, 8)),
             dma((4, 4, 8)), dma((4, 4, 8)),
             dma((4, 4)), dma((4, 4)),
             dma((2, 3, 2, 4)), dma((2, 3, 2, 4)),
-            dma, dma,
+            dma, dma((8,)),
         ],
         compiler_params=pltpu.CompilerParams(
-            collective_id=0, has_side_effects=True, vmem_limit_bytes=56 << 20
+            collective_id=0, has_side_effects=True, vmem_limit_bytes=58 << 20
         ),
         name="fronts",
-    )(inv, cross, contrib, csrc, psrc, emap)
-
-
-def spread_kernel(start, target, index, rows, parent, rhs, front, right, tile):
-    i = pl.program_id(0)
-
-    @pl.when(i == 0)
-    def _():
-        front[...] = parent[...]
-        right[...] = rhs[...]
-
-    row = lax.broadcasted_iota(I32, (56, 64), 0)
-    pick = [(row == target[v, 0]).astype(F32).astype(BF16) for v in range(4)]
-    tail = jnp.zeros((56, 256), F32)
-    for q in range(3):
-        got = rows[0, :, 256 * q : 256 * (q + 1)]
-        main = dot(pick[0], got)
-        tile[2 * q] = main[:, :128]
-        tile[2 * q + 1] = main[:, 128:]
-        tail = tail + dot(pick[q + 1], got)
-    tile[6] = tail[:, :128]
-    tile[7] = tail[:, 128:]
-    which = lax.rem(i, 4)
-    for zz in range(4):
-
-        @pl.when(which == zz)
-        def _():
-            right[:, 128 * zz : 128 * (zz + 1)] += tail[:, 128:]
-
-    lane = lax.broadcasted_iota(I32, (56, 128), 1)
-    for t in range(56):
-        at = start[i, t]
-        j = at // 128
-        both = jnp.where(lane >= lax.rem(at, 128), tile[j], tile[j + 1])
-        where = jnp.broadcast_to(index[0, t : t + 1], (56, 128))
-        taken = jnp.take_along_axis(both, where & 127, axis=1)
-        front[:, 128 * t : 128 * (t + 1)] += jnp.where(where >= 0, taken, 0.0)
-
-
-def spread(start, target, index, rows, parent, rhs):
-    whole = lambda shape: pl.BlockSpec(shape, lambda i: (0,) * len(shape))
-    return pl.pallas_call(
-        spread_kernel,
-        grid=(32,),
-        out_shape=(
-            jax.ShapeDtypeStruct((56, 7168), F32),
-            jax.ShapeDtypeStruct((56, 512), F32),
-        ),
-        in_specs=[
-            pl.BlockSpec(memory_space=pltpu.SMEM),
-            pl.BlockSpec((4, 1, 1, 64), lambda i: (0, i // 4, 0, 0)),
-            pl.BlockSpec((1, 56, 128), lambda i: (i, 0, 0)),
-            pl.BlockSpec((1, 64, 768), lambda i: (i, 0, 0)),
-            whole((56, 7168)),
-            whole((56, 512)),
-        ],
-        out_specs=(whole((56, 7168)), whole((56, 512))),
-        scratch_shapes=[pltpu.VMEM((8, 56, 128), F32)],
-        compiler_params=pltpu.CompilerParams(vmem_limit_bytes=40 << 20),
-        name="spread",
-    )(start, target, index, rows, parent, rhs)
+    )(inv, cross, contrib, csrc, psrc, emap, parent, rhs)
 
 
 def on_device(
     pivot_inverse, cross_block, contrib_block, pivot_sources, contrib_sources, ext_map, parent_front, parent_rhs
 ):
-    emap = jnp.broadcast_to(ext_map, (8, 224))
-    arrived, index, start, target, solved_own = main_call(
-        pivot_inverse[0], cross_block[0], contrib_block[0], contrib_sources[0], pivot_sources[0], emap
+    front, right, solved_own = main_call(
+        pivot_inverse[0], cross_block[0], contrib_block[0], contrib_sources[0], pivot_sources[0],
+        jnp.broadcast_to(ext_map, (8, 224)), parent_front, parent_rhs,
     )
-    solved = solved_own.transpose(1, 0, 2).reshape(1, 128, 512)
-    front, right = spread(
-        start[:, 0, :], target.reshape(4, 8, 1, 64), index, arrived.reshape(32, 64, 768), parent_front, parent_rhs
-    )
-    return solved, front, right
+    return solved_own.transpose(1, 0, 2).reshape(1, 128, 512), front, right
 
 
 def solution(mesh):

time: 188 us -> 167 us (0.89)
  Pallas kernels: 179 us -> 160 us
    pallas_call x2 -> x1, Pallas kernels: 179 us -> 160 us  [main_call(): pl.pallas_call(main_kernel, out_shape=(jax.ShapeDtypeStruct((56, 7168), F...]
    unnamed x11 -> x5, local copies, waits for them, and re-layouts: 4.56 us -> 4.13 us
where the time goes in v2:
time: 167 us
  Pallas kernels  160 us (96%)
  local copies, waits for them, and re-layouts  6.43 us (4%)
    pallas_call x1, Pallas kernels, main_call(): pl.pallas_call(main_kernel, out_shape=(jax.ShapeDtypeStruct((56, 7168), F...  160 us
    unnamed x5, local copies, waits for them, and re-layouts  4.13 us

profile of v2, /device:TPU:1, one launch (start us, length us, event | category | flops | bytes accessed | tf_op | source)
XLA Modules:
  0.0 166.7 jit_solution(5225306855101959392)
XLA Ops:
  0.6 1.3 broadcast_in_dim.8.emap
  1.9 159.6 %fronts.1 = (f32[56,7168]{1,0:T(8,128)}, f32[56,512]{1,0:T(8,128)}, bf16[4,128,128]{2,1,0:T(8,128)(2,1)}) custom-call(bf16[128,2048]{1,0:T(8,128)(2,1)} %bitcast.10, bf16[224,2048]{1,0:T(8,128)(2,1)} %bitcast.9, f32[224,3584]{1,0:T(8,128)} %bitcast.8, bf16[224,512]{1,0:T(8,128)(2,1)} %bitcast.12, bf16[128,512]{1,0:T(8,128)(2,1)} %bitcast.13, ...), custom_call_target="tpu_custom_call" | custom-call | tf_op jit(solution)/shard_map/fronts/pallas_call | solution.py:497
  161.5 1.0 copy.11
  162.5 0.8 copy.12
  163.3 0.0 copy-start
  163.3 2.7 %copy.15 = f32[56,7168]{1,0:T(8,128)} copy(f32[56,7168]{1,0:T(8,128)} %get-tuple-element.16) | data formatting | bytes 3211264
  166.0 0.0 copy-done
  166.0 0.6 copy.16
Async XLA Ops:
  163.3 2.7 %copy-start = (f32[56,512]{1,0:T(8,128)S(1)}, f32[56,512]{1,0:T(8,128)}, u32[]{:S(2)}) copy-start(f32[56,512]{1,0:T(8,128)} %get-tuple-element.17) | copy-start | bytes 344068

commit v3 on v2

--- a/solution.py
+++ b/solution.py
@@ -11,7 +11,7 @@
 F32, BF16, I32 = jnp.float32, jnp.bfloat16, jnp.int32
 NT = (((1,), (1,)), ((), ()))
 NN = (((1,), (0,)), ((), ()))
-UNROLL = 8
+UNROLL = 14
 
 
 def dot(a, b, dims=NN):
@@ -66,7 +66,7 @@
     inv, cross, contrib, csrc, psrc, emap, parent, rhs,
     front, right, solved_own,
     invf, srcb, low, la, lb, cbuf, sent, held, solved_all, moved, select, slots, outs, mapsb,
-    arrived, index, start, start_at, target, tile,
+    arrived, index, start, start_at, target, tile, via, vs, vr,
     loc_sem, ms, mr, zs, zr, xs, xr, cs, cr, ls, lr, es, er,
 ):
     g = lax.axis_index("grp")
@@ -123,7 +123,7 @@
 
     each(16, clear)
     own.start()
-    mapsb[pl.ds(pl.multiple_of(me * 8, 8), 8), :] = emap[...]
+    mapsb[pl.ds(pl.multiple_of(me * 8, 8), 8), :] = jnp.broadcast_to(emap[...], (8, 224))
     for b in range(4):
         @pl.when(z == b)
         def _():
@@ -136,53 +136,56 @@
     own.wait()
     pl.semaphore_wait(barrier, 127)
 
-    def piece(block, c, part=None):
-        cols = pl.ds(pl.multiple_of(c * 256, 256), 256)
-        if part is None:
-            return invf.at[block, :, cols]
-        return invf.at[block, pl.ds(64 * part, 64), cols]
+    def sized(block, fn):
+        for n in range(1, 9):
+            pl.when(chunks(block) == n)(functools.partial(fn, 256 * n))
+
+    def piece(block, n, part):
+        return invf.at[block, pl.ds(64 * part, 64), pl.ds(0, n)]
 
     def map_rows(first, count):
         return mapsb.at[pl.ds(pl.multiple_of(first * 8, 8), count * 8), :]
 
-    def send_z(c):
-        remote(piece(h, c), piece(h, c), zs.at[0, c], zr.at[0, c], at(1, 0)).start()
-        remote(piece(h, c), piece(h, c), zs.at[1, c], zr.at[1, c], at(-1, 0)).start()
-
-    def send_x(r, block):
-        def go(c):
-            remote(piece(block, c), piece(block, c), xs.at[r, 0, c], xr.at[r, 0, c], at(0, 1)).start()
-            remote(piece(block, c), piece(block, c), xs.at[r, 1, c], xr.at[r, 1, c], at(0, -1)).start()
-
-        return go
-
-    def pass_z(block, d, step):
-        def go(c):
-            wait(piece(block, c), zr.at[d, c])
-            remote(
-                piece(block, c, d), piece(block, c, d), zs.at[2 + d, c], zr.at[2 + d, c], at(step, 0)
-            ).start()
-
-        return go
+    def send(block, part, ssem, rsem, to):
+        def go(n):
+            ref = piece(block, n, part)
+            remote(ref, ref, ssem, rsem, to).start()
+
+        sized(block, go)
+
+    def await_piece(block, part, sem):
+        sized(block, lambda n: wait(piece(block, n, part), sem))
+
+    def send_both(block, ssem, rsem, right, left, parts):
+        def go(n):
+            for p in parts:
+                for d, to in ((0, right), (1, left)):
+                    part = p if d == 0 or len(parts) == 1 else 1 - p
+                    ref = piece(block, n, part)
+                    remote(ref, ref, ssem.at[d, part], rsem.at[d, part], to).start()
+
+        sized(block, go)
 
     offsets = (0, -1, 1, 2)
+
+    def send_x(r, parts=(0, 1)):
+        send_both(at(offsets[r], 0), xs.at[r], xr.at[r], at(0, 1), at(0, -1), parts)
 
     def pass_x(r):
         for d, dx in ((0, -1), (1, 1)):
             block = at(offsets[r], dx)
 
-            def go(c, d=d, dx=dx, block=block):
-                wait(piece(block, c), xr.at[r, d, c])
-                remote(
-                    piece(block, c, d), piece(block, c, d), xs.at[r, 2 + d, c], xr.at[r, 2 + d, c], at(0, -dx)
-                ).start()
-
-            each(chunks(block), go)
+            def go(n, d=d, dx=dx, block=block):
+                ref = piece(block, n, d)
+                wait(ref, xr.at[r, d, d])
+                remote(ref, ref, xs.at[r, 2 + d, 0], xr.at[r, 2 + d, 0], at(0, -dx)).start()
+
+            sized(block, go)
 
     for i in (1, 2, 3):
         remote(map_rows(me, 1), map_rows(me, 1), ms.at[0, i], mr.at[0, i], at(0, i)).start()
-    each(chunks(h), send_z)
-    each(chunks(h), send_x(0, h))
+    send_both(h, zs, zr, at(1, 0), at(-1, 0), (0, 1))
+    send_x(0)
     for i in (1, 2, 3):
         to = lax.rem(z + i, 4)
         cols = pl.ds(pl.multiple_of(to * 128, 128), 128)
@@ -193,19 +196,19 @@
     for i in (1, 2, 3):
         remote(map_rows(line, 4), map_rows(line, 4), ms.at[1, i], mr.at[1, i], at(i, 0)).start()
 
-    def first(c):
-        pass_z(at(-1, 0), 0, 1)(c)
-        send_x(1, at(-1, 0))(c)
-
-    def second(c):
-        pass_z(at(1, 0), 1, -1)(c)
-        send_x(2, at(1, 0))(c)
-
-    each(chunks(at(-1, 0)), first)
-    each(chunks(at(1, 0)), second)
-    for i in (1, 2, 3):
-        to = lax.rem(z + i, 4)
-        remote(sent.at[to], held.at[z], cs.at[1, i], cr.at[1, i], at(i, 0)).start()
+    for d, dz in ((0, -1), (1, 1)):
+        block = at(dz, 0)
+        await_piece(block, d, zr.at[d, d])
+        send(block, d, zs.at[2 + d, 0], zr.at[2 + d, 0], at(-dz, 0))
+        send_x(1 + d, (d,))
+    for d, dz in ((0, -1), (1, 1)):
+        await_piece(at(dz, 0), 1 - d, zr.at[d, 1 - d])
+        send_x(1 + d, (1 - d,))
+    for d, i in ((0, 1), (1, 3)):
+        part = pl.ds(112 * d, 112)
+        remote(sent.at[lax.rem(z + 2, 4), part, :], via.at[d], vs.at[0, d], vr.at[0, d], at(i, 0)).start()
+    for i in (1, 3):
+        remote(sent.at[lax.rem(z + i, 4)], held.at[z], cs.at[1, i], cr.at[1, i], at(i, 0)).start()
     own_sent = pltpu.make_async_copy(sent.at[z], held.at[z], loc_sem.at[2])
     own_sent.start()
     for i in (1, 2, 3):
@@ -218,15 +221,12 @@
     pass_x(0)
     for i in (1, 2, 3):
         wait(srcb.at[z, x], cr.at[0, i])
-    for i in (1, 2, 3):
+    for i in (1, 3):
         remote(srcb.at[:, x], srcb.at[:, x], cs.at[2, i], cr.at[2, i], at(0, i)).start()
 
-    def third(c):
-        wait(piece(at(2, 0), c, 0), zr.at[2, c])
-        wait(piece(at(2, 0), c, 1), zr.at[3, c])
-        send_x(3, at(2, 0))(c)
-
-    each(chunks(at(2, 0)), third)
+    for d in (0, 1):
+        await_piece(at(2, 0), d, zr.at[2 + d, 0])
+        send_x(3, (d,))
     pass_x(1)
 
     rings = ((la, z, 1, 0), (lb, x, 0, 1))
@@ -240,11 +240,10 @@
     def factor(r):
         block = at(offsets[r], 2)
 
-        def arrive(c):
-            wait(piece(block, c, 0), xr.at[r, 2, c])
-            wait(piece(block, c, 1), xr.at[r, 3, c])
-
-        each(chunks(block), arrive)
+        await_piece(at(offsets[r], -1), 1, xr.at[r, 0, 1])
+        await_piece(at(offsets[r], 1), 0, xr.at[r, 1, 0])
+        await_piece(block, 0, xr.at[r, 2, 0])
+        await_piece(block, 1, xr.at[r, 3, 0])
         zz = lax.rem(z + offsets[r] + 4, 4)
         for part in range(2):
             m = 2 * zz + part
@@ -276,11 +275,21 @@
         index[i] = jnp.where(member > 0.5, lax.rem(place, 128), -1)[:56]
         start[i] = jnp.clip(starts, 0, 895)
 
+    for d, i in ((0, 1), (1, 3)):
+        wait(via.at[d], vr.at[0, d])
+        origin = lax.rem(z + 4 - i, 4)
+        remote(
+            via.at[d], held.at[origin, pl.ds(112 * d, 112), :], vs.at[1, d], vr.at[1, d], at(i, 0)
+        ).start()
     factor(0)
     for i in range(1, 8):
         wait(map_rows(0, 16), mr.at[2, i])
     each(8, table)
     pass_x(2)
+    for d, i in ((0, 1), (1, 3)):
+        wait(srcb.at[:, x], cr.at[2, i])
+        ref = srcb.at[pl.ds(2 * d, 2), lax.rem(x + 4 - i, 4)]
+        remote(ref, ref, vs.at[2, d], vr.at[2, d], at(0, i)).start()
     factor(1)
     factor_pass(0)
     each(16, table, 8)
@@ -306,18 +315,19 @@
         slot_ids.append(jnp.broadcast_to(pos + 3 * k, (8, 224)))
     owner, slot = joined(owners)[0:1], joined(slot_ids)[0:1]
     slots[0:1] = owner * 16 + slot
-    for q in range(3):
-        slots[q + 1 : q + 2] = jnp.where(slot // 4 == q, owner * 16 + 12 + lax.rem(slot, 4), -1)
 
     factor(2)
     factor_pass(1)
     each(24, table, 16)
-    for i in (1, 2, 3):
-        wait(srcb.at[:, x], cr.at[2, i])
+    for d in (0, 1):
+        ref = srcb.at[pl.ds(2 * d, 2), x]
+        wait(ref, vr.at[2, d])
     factor(3)
     factor_pass(2)
     sources = srcb[...].reshape(2048, 128)
 
+    own_part = solved_own.at[:, pl.ds(pl.multiple_of(z * 128, 128), 128)]
+
     def solve(m):
         rows = invf[pl.ds(2 * m, 2)].reshape(256, 2048)
         solved_all[pl.ds(pl.multiple_of(m * 256, 256), 256), :] = dot(rows, sources).astype(BF16)
@@ -326,11 +336,11 @@
     for i in (1, 2, 3):
         to = at(i, 0)
         remote(
-            solved_all.at[pl.ds(pl.multiple_of(to * 128, 128), 128), :], solved_own.at[z],
+            solved_all.at[pl.ds(pl.multiple_of(to * 128, 128), 128), :], own_part,
             cs.at[3, i], cr.at[3, i], to,
         ).start()
     own_s = pltpu.make_async_copy(
-        solved_all.at[pl.ds(pl.multiple_of(h * 128, 128), 128), :], solved_own.at[z], loc_sem.at[3]
+        solved_all.at[pl.ds(pl.multiple_of(h * 128, 128), 128), :], own_part, loc_sem.at[3]
     )
     own_s.start()
     la[z] = low[...]
@@ -366,8 +376,10 @@
         target[v] = totals[v].astype(I32) - 1
 
     factor_pass(3)
-    for i in (1, 2, 3):
+    for i in (1, 3):
         wait(held.at[z], cr.at[1, i])
+    for d in (0, 1):
+        wait(via.at[d], vr.at[1, d])
     own_sent.wait()
     for r in range(4):
         for a, (ref, mine, dz, dx) in enumerate(rings):
@@ -388,11 +400,17 @@
         grp = lax.rem(g + j, 8)
         row = lax.broadcasted_iota(I32, (256, 896), 0) + grp * 256
         main = (row == slots[0:1]).astype(F32).astype(BF16)
-        last = moved[:, :, 768:1024].reshape(896, 256)
-        for q in range(3):
-            extra = (row == slots[q + 1 : q + 2]).astype(F32).astype(BF16)
-            part = dot(main, moved[:, :, 256 * q : 256 * (q + 1)].reshape(896, 256)) + dot(extra, last)
-            outs[pl.ds(grp * 16, 16), :, 256 * q : 256 * (q + 1)] = part.astype(BF16).reshape(16, 16, 256)
+        def quarter(q):
+            cols = moved[:, :, 256 * q : 256 * (q + 1)].reshape(896, 256)
+            return dot(main, cols).reshape(16, 2, 8, 256)
+
+        last = quarter(3)
+        free = lax.broadcasted_iota(I32, (16, 8, 256), 1) >= 4
+        turned = [jnp.concatenate([last[:, t, 4:], last[:, t, :4]], axis=1) for t in range(2)]
+        for q, extra in enumerate((turned[0], last[:, 0], turned[1])):
+            part = quarter(q)
+            both = jnp.concatenate([part[:, 0], jnp.where(free, extra, part[:, 1])], axis=1)
+            outs[pl.ds(grp * 16, 16), :, 256 * q : 256 * (q + 1)] = both.astype(BF16)
 
         def go(i):
             to = lax.rem(h + i, 16)
@@ -448,38 +466,25 @@
 
     each(8, spread)
 
-    def sent_z(c):
-        for d in (0, 1):
-            wait(piece(h, c), zs.at[d, c])
-
-    each(chunks(h), sent_z)
-    for d, dz in ((0, -1), (1, 1)):
-
-        def sent_pass(c, d=d, dz=dz):
-            wait(piece(at(dz, 0), c, d), zs.at[2 + d, c])
-
-        each(chunks(at(dz, 0)), sent_pass)
-    for r in range(4):
-
-        def sent_x(c, r=r):
-            for d in (0, 1):
-                wait(piece(at(offsets[r], 0), c), xs.at[r, d, c])
-
-        each(chunks(at(offsets[r], 0)), sent_x)
-        for d, dx in ((0, -1), (1, 1)):
-
-            def sent_pass_x(c, r=r, d=d, dx=dx):
-                wait(piece(at(offsets[r], dx), c, d), xs.at[r, 2 + d, c])
-
-            each(chunks(at(offsets[r], dx)), sent_pass_x)
+    for d in (0, 1):
+        for part in (0, 1):
+            await_piece(h, part, zs.at[d, part])
+            for r in range(4):
+                await_piece(at(offsets[r], 0), part, xs.at[r, d, part])
+        step = 2 * d - 1
+        await_piece(at(step, 0), d, zs.at[2 + d, 0])
+        for r in range(4):
+            await_piece(at(offsets[r], step), d, xs.at[r, 2 + d, 0])
     for i in (1, 2, 3):
         wait(map_rows(me, 1), ms.at[0, i])
         wait(map_rows(line, 4), ms.at[1, i])
         wait(srcb.at[z, x], cs.at[0, i])
-        wait(held.at[z], cs.at[1, i])
-        wait(srcb.at[:, x], cs.at[2, i])
-        wait(solved_own.at[z], cs.at[3, i])
-        wait(solved_own.at[z], cr.at[3, i])
+        if i != 2:
+            wait(held.at[z], cs.at[1, i])
+        if i != 2:
+            wait(srcb.at[:, x], cs.at[2, i])
+        wait(own_part, cs.at[3, i])
+        wait(own_part, cr.at[3, i])
     for i in range(1, 8):
         wait(map_rows(0, 16), ms.at[2, i])
     for r in range(4):
@@ -488,6 +493,10 @@
                 for part in (0, 1):
                     wait(lpart(ref, mine_at, part, r), ls.at[a, d, part, r])
                 wait(lpart(ref, mine_at, d, r), ls.at[a, 2, d, r])
+    for d in (0, 1):
+        wait(via.at[d], vs.at[0, d])
+        wait(via.at[d], vs.at[1, d])
+        wait(srcb.at[pl.ds(2 * d, 2), x], vs.at[2, d])
     own_s.wait()
     wait(outs.at[pl.ds(0, 127)], es)
 
@@ -499,7 +508,7 @@
         out_shape=(
             jax.ShapeDtypeStruct((56, 7168), F32),
             jax.ShapeDtypeStruct((56, 512), F32),
-            jax.ShapeDtypeStruct((4, 128, 128), BF16),
+            jax.ShapeDtypeStruct((128, 512), BF16),
         ),
         in_specs=[hbm(), vmem(), hbm(), vmem(), vmem(), vmem(), hbm(), hbm()],
         out_specs=(vmem(), vmem(), hbm()),
@@ -524,10 +533,12 @@
             pltpu.SMEM((32, 8, 64), I32),
             pltpu.VMEM((4, 8, 64), I32),
             pltpu.VMEM((4, 8, 56, 128), F32),
+            pltpu.VMEM((2, 112, 1024), BF16),
+            dma((3, 2)), dma((3, 2)),
             dma((8,)),
             dma((3, 8)), dma((3, 8)),
-            dma((4, 8)), dma((4, 8)),
-            dma((4, 4, 8)), dma((4, 4, 8)),
+            dma((4, 2)), dma((4, 2)),
+            dma((4, 4, 2)), dma((4, 4, 2)),
             dma((4, 4)), dma((4, 4)),
             dma((2, 3, 2, 4)), dma((2, 3, 2, 4)),
             dma, dma((8,)),
@@ -544,9 +555,9 @@
 ):
     front, right, solved_own = main_call(
         pivot_inverse[0], cross_block[0], contrib_block[0], contrib_sources[0], pivot_sources[0],
-        jnp.broadcast_to(ext_map, (8, 224)), parent_front, parent_rhs,
+        ext_map, parent_front, parent_rhs,
     )
-    return solved_own.transpose(1, 0, 2).reshape(1, 128, 512), front, right
+    return solved_own[None], front, right
 
 
 def solution(mesh):

time: 167 us -> 163 us (0.976)
  Pallas kernels: 160 us -> 156 us
    pallas_call x1, Pallas kernels: 160 us -> 156 us  [main_call(): pl.pallas_call(main_kernel, out_shape=(jax.ShapeDtypeStruct((56, 7168), F...]
where the time goes in v3:
time: 163 us; the launch traced here: 162 us
  Pallas kernels  156 us (96%)
  local copies, waits for them, and re-layouts  4.93 us (3%)
    pallas_call x1, Pallas kernels, main_call(): pl.pallas_call(main_kernel, out_shape=(jax.ShapeDtypeStruct((56, 7168), F...  156 us
    unnamed x5, local copies, waits for them, and re-layouts  4.93 us

profile of v3, /device:TPU:1, one launch (start us, length us, event | category | flops | bytes accessed | tf_op | source)
XLA Modules:
  0.0 161.8 jit_solution(15068051348107881567)
XLA Ops:
  0.6 156.2 %fronts.1 = (f32[56,7168]{1,0:T(8,128)}, f32[56,512]{1,0:T(8,128)}, bf16[128,512]{1,0:T(8,128)(2,1)}) custom-call(bf16[128,2048]{1,0:T(8,128)(2,1)} %bitcast.8, bf16[224,2048]{1,0:T(8,128)(2,1)} %bitcast.7, f32[224,3584]{1,0:T(8,128)} %bitcast.6, bf16[224,512]{1,0:T(8,128)(2,1)} %bitcast.9, bf16[128,512]{1,0:T(8,128)(2,1)} %bitcast.10, s32[1,224]{1,0:T(1,128)} %emap.1, ...), custom_call_target="tpu_custom_call" | custom-call | tf_op jit(solution)/shard_map/fronts/pallas_call | solution.py:506
  156.8 1.6 copy.14
  158.4 0.0 copy-start
  158.4 2.7 %copy.15 = f32[56,7168]{1,0:T(8,128)} copy(f32[56,7168]{1,0:T(8,128)} %get-tuple-element.13) | data formatting | bytes 3211264
  161.1 0.0 copy-done
  161.1 0.6 copy.16
Async XLA Ops:
  158.4 2.7 %copy-start = (f32[56,512]{1,0:T(8,128)S(1)}, f32[56,512]{1,0:T(8,128)}, u32[]{:S(2)}) copy-start(f32[56,512]{1,0:T(8,128)} %get-tuple-element.14) | copy-start | bytes 344068

commit v4 on v3

--- a/solution.py
+++ b/solution.py
@@ -452,15 +452,15 @@
             for u in range(UNROLL):
                 t = s * UNROLL + u
                 cols = pl.ds(pl.multiple_of(t * 128, 128), 128)
-                total = front[:, cols]
+                total = jnp.zeros((56, 128), F32)
                 for b in range(4):
                     begin = start_at[grp * 4 + b, 0, t]
                     i = jnp.clip(begin // 128, 0, 6)
                     both = jnp.where(lane >= lax.rem(begin, 128), tile[b, i], tile[b, i + 1])
                     where = jnp.broadcast_to(index[grp * 4 + b, pl.ds(t, 1), :], (56, 128))
                     taken = jnp.take_along_axis(both, where & 127, axis=1)
-                    total = total + jnp.where(where >= 0, taken, 0.0)
-                front[:, cols] = total
+                    total = jnp.where(where >= 0, taken, total)
+                front[:, cols] += total
 
         each(56 // UNROLL, columns)
 

time: 163 us -> 163 us (level)
  no operation moved by 1% of the time
where the time goes in v4:
time: 163 us; the launch traced here: 162 us
  Pallas kernels  156 us (96%)
  local copies, waits for them, and re-layouts  4.93 us (3%)
    pallas_call x1, Pallas kernels, main_call(): pl.pallas_call(main_kernel, out_shape=(jax.ShapeDtypeStruct((56, 7168), F...  156 us
    unnamed x5, local copies, waits for them, and re-layouts  4.93 us

profile of v4, /device:TPU:1, one launch (start us, length us, event | category | flops | bytes accessed | tf_op | source)
XLA Modules:
  0.0 161.8 jit_solution(15827372067237280238)
XLA Ops:
  0.6 156.2 %fronts.1 = (f32[56,7168]{1,0:T(8,128)}, f32[56,512]{1,0:T(8,128)}, bf16[128,512]{1,0:T(8,128)(2,1)}) custom-call(bf16[128,2048]{1,0:T(8,128)(2,1)} %bitcast.8, bf16[224,2048]{1,0:T(8,128)(2,1)} %bitcast.7, f32[224,3584]{1,0:T(8,128)} %bitcast.6, bf16[224,512]{1,0:T(8,128)(2,1)} %bitcast.9, bf16[128,512]{1,0:T(8,128)(2,1)} %bitcast.10, s32[1,224]{1,0:T(1,128)} %emap.1, ...), custom_call_target="tpu_custom_call" | custom-call | tf_op jit(solution)/shard_map/fronts/pallas_call | solution.py:506
  156.8 1.6 copy.14
  158.4 0.0 copy-start
  158.4 2.7 %copy.15 = f32[56,7168]{1,0:T(8,128)} copy(f32[56,7168]{1,0:T(8,128)} %get-tuple-element.13) | data formatting | bytes 3211264
  161.1 0.0 copy-done
  161.1 0.6 copy.16
Async XLA Ops:
  158.4 2.7 %copy-start = (f32[56,512]{1,0:T(8,128)S(1)}, f32[56,512]{1,0:T(8,128)}, u32[]{:S(2)}) copy-start(f32[56,512]{1,0:T(8,128)} %get-tuple-element.14) | copy-start | bytes 344068

commit v5 on v4

--- a/solution.py
+++ b/solution.py
@@ -284,7 +284,6 @@
     factor(0)
     for i in range(1, 8):
         wait(map_rows(0, 16), mr.at[2, i])
-    each(8, table)
     pass_x(2)
     for d, i in ((0, 1), (1, 3)):
         wait(srcb.at[:, x], cr.at[2, i])
@@ -292,7 +291,7 @@
         remote(ref, ref, vs.at[2, d], vr.at[2, d], at(0, i)).start()
     factor(1)
     factor_pass(0)
-    each(16, table, 8)
+    each(8, table)
     pass_x(3)
 
     own_maps = [mapsb[pl.ds(pl.multiple_of((line + b) * 8, 8), 8), :] for b in range(4)]
@@ -318,7 +317,7 @@
 
     factor(2)
     factor_pass(1)
-    each(24, table, 16)
+    each(16, table, 8)
     for d in (0, 1):
         ref = srcb.at[pl.ds(2 * d, 2), x]
         wait(ref, vr.at[2, d])
@@ -345,7 +344,7 @@
     own_s.start()
     la[z] = low[...]
     lb[x] = low[...]
-    each(32, table, 24)
+    each(32, table, 16)
     starts_in = pltpu.make_async_copy(start, start_at, loc_sem.at[7])
     starts_in.start()
 

time: 163 us -> 168 us (1.031)
  Pallas kernels: 156 us -> 161 us
    pallas_call x1, Pallas kernels: 156 us -> 161 us  [main_call(): pl.pallas_call(main_kernel, out_shape=(jax.ShapeDtypeStruct((56, 7168), F...]
where the time goes in v5:
time: 168 us; the launch traced here: 167 us
  Pallas kernels  161 us (96%)
  local copies, waits for them, and re-layouts  4.93 us (3%)
    pallas_call x1, Pallas kernels, main_call(): pl.pallas_call(main_kernel, out_shape=(jax.ShapeDtypeStruct((56, 7168), F...  161 us
    unnamed x5, local copies, waits for them, and re-layouts  4.93 us

profile of v5, /device:TPU:1, one launch (start us, length us, event | category | flops | bytes accessed | tf_op | source)
XLA Modules:
  0.0 166.6 jit_solution(4114106657520142874)
XLA Ops:
  0.6 161.0 %fronts.1 = (f32[56,7168]{1,0:T(8,128)}, f32[56,512]{1,0:T(8,128)}, bf16[128,512]{1,0:T(8,128)(2,1)}) custom-call(bf16[128,2048]{1,0:T(8,128)(2,1)} %bitcast.8, bf16[224,2048]{1,0:T(8,128)(2,1)} %bitcast.7, f32[224,3584]{1,0:T(8,128)} %bitcast.6, bf16[224,512]{1,0:T(8,128)(2,1)} %bitcast.9, bf16[128,512]{1,0:T(8,128)(2,1)} %bitcast.10, s32[1,224]{1,0:T(1,128)} %emap.1, ...), custom_call_target="tpu_custom_call" | custom-call | tf_op jit(solution)/shard_map/fronts/pallas_call | solution.py:505
  161.7 1.6 copy.14
  163.2 0.0 copy-start
  163.2 2.7 %copy.15 = f32[56,7168]{1,0:T(8,128)} copy(f32[56,7168]{1,0:T(8,128)} %get-tuple-element.13) | data formatting | bytes 3211264
  165.9 0.0 copy-done
  165.9 0.6 copy.16
Async XLA Ops:
  163.2 2.7 %copy-start = (f32[56,512]{1,0:T(8,128)S(1)}, f32[56,512]{1,0:T(8,128)}, u32[]{:S(2)}) copy-start(f32[56,512]{1,0:T(8,128)} %get-tuple-element.14) | copy-start | bytes 344068
